TPU v7x, 256 devices: a whole 4x4x8 slice. The times are simulated.
256 devices in a mesh: frame: 8 (over z), tile: 32 (over x, y, core).
Axes of the slice: x: 4, y: 4, z: 8, core: 2. Of those that a mesh axis runs over, the one named last changes fastest.
Arguments:
- displacement: bfloat16 [512, 2, 32, 4096], P('frame', None, 'tile'), may hold values from -256 to 256
Outputs:
- basis: bfloat16 [512, 3, 32, 4096], P(None, None, 'tile', 'frame')
- factor: float32 [512, 512], replicated
All inputs are finite; a program needn't handle non-finite values.
Results may differ from a plain program's by a relative error of at most 0.0053.
The roundings to bfloat16 on the way count: a program that leaves them out, or rounds other values in their place, can miss the bound.
Values may be sent and summed in bfloat16 or wider, within the bound.
No kernel may reach another device: no remote copies, remote signals or barrier semaphores. Data moves between devices by JAX's collectives and lax.ppermute only.
A program may use at most 64 MiB of HBM per device.

v0:
```python
import math
import jax
import jax.numpy as jnp
from jax import lax
from jax.sharding import PartitionSpec as P


def with_halo(array, sides, width):
    for axis, dim in sides:
        peers, length = (lax.axis_size(axis), array.shape[dim])
        up = [(i, (i + 1) % peers) for i in range(peers - 1)]
        down = [(j, i) for i, j in up]
        last = lax.slice_in_dim(array, length - width, length, axis=dim)
        first = lax.slice_in_dim(array, 0, width, axis=dim)
        before = lax.ppermute(last, axis, up)
        after = lax.ppermute(first, axis, down)
        array = jnp.concatenate([before, array, after], axis=dim)
    return array


def derivative(center, before, after, first, final):
    return jnp.where(
        first, after - center, jnp.where(final, center - before, (after - before) * 0.5)
    )


def column_derivative(center):
    width = center.shape[-1]
    after = jnp.concatenate([center[..., 1:], center[..., -1:]], axis=-1)
    before = jnp.concatenate([center[..., :1], center[..., :-1]], axis=-1)
    column = jnp.arange(width, dtype=jnp.int32)
    return derivative(center, before, after, column == 0, column == width - 1)


def combine_strain(d_rows, d_cols):
    return jnp.stack(
        [d_cols[:, 0], d_rows[:, 1], 0.5 * (d_rows[:, 0] + d_cols[:, 1])], axis=1
    ).astype(jnp.bfloat16)


def local(displacement):
    rows = displacement.shape[2]
    full_width = displacement.shape[3]
    total_rows = lax.axis_size("tile") * rows
    scale = math.sqrt(3 * total_rows * full_width)
    row_global = lax.axis_index("tile") * rows + jnp.arange(rows, dtype=jnp.int32)
    first = (row_global == 0)[:, None]
    final = (row_global == total_rows - 1)[:, None]
    padded = with_halo(displacement, (("tile", 2),), 1)
    field = padded.astype(jnp.float32)
    center = field[:, :, 1:-1, :]
    d_rows = derivative(center, field[:, :, :-2, :], field[:, :, 2:, :], first, final)
    d_cols = column_derivative(center)
    strain = combine_strain(d_rows, d_cols)
    pixel_major = lax.all_to_all(strain, "frame", split_axis=3, concat_axis=0, tiled=True)
    frames = pixel_major.shape[0]
    snapshot_half = pixel_major.reshape(frames, -1)
    local_gram = lax.dot_general(
        snapshot_half, snapshot_half, (((1,), (1,)), ((), ())), preferred_element_type=jnp.float32
    )
    gram = lax.psum(local_gram, ("frame", "tile"))
    lower = jnp.linalg.cholesky(gram)
    snapshot = snapshot_half.astype(jnp.float32)
    solved = lax.linalg.triangular_solve(lower, snapshot, left_side=True, lower=True)
    basis = (solved * scale).astype(jnp.bfloat16).reshape(pixel_major.shape)
    return (basis, lower.T / scale)


def solution(mesh):
    return jax.shard_map(
        local,
        mesh=mesh,
        in_specs=(P("frame", None, "tile", None),),
        out_specs=(P(None, None, "tile", "frame"), P()),
        check_vma=False,
    )
```

profile of v0, /device:TPU:2, one launch (start us, length us, event | category | flops | bytes accessed | tf_op | source)
XLA Modules:
  0.0 526.9 jit_solution(18431249091505621572)
XLA Ops:
  7.2 1.8 copy.46
  9.0 1.9 collective-permute-start
  10.9 5.8 %collective-permute-start.1 = (bf16[64,2,1,4096]{3,0,2,1:T(8,128)(2,1)S(1)}, bf16[64,2,1,4096]{3,0,2,1:T(8,128)(2,1)S(1)}, u32[]{:S(2)}, u32[]{:S(2)}) collective-permute-start(bf16[64,2,1,4096]{3,0,2,1:T(8,128)(2,1)S(1)} %copy.46), channel_id=1, source_target_pairs={{1,0},{2,1},{3,2},{4,3},{5,4},{6,5},{7,6},{8,7},{9,8},{10,9},{11,1... | collective-permute-start | bytes 3145736 | tf_op jit(solution)/shard_map/ppermute | solution.py:16
  16.7 10.5 %collective-permute-done = bf16[64,2,1,4096]{3,0,2,1:T(8,128)(2,1)S(1)} collective-permute-done((bf16[64,2,1,4096]{3,0,2,1:T(8,128)(2,1)S(1)}, bf16[64,2,1,4096]{3,0,2,1:T(8,128)(2,1)S(1)}, u32[]{:S(2)}, u32[]{:S(2)}) %collective-permute-start) | collective-permute-done | bytes 1048608 | tf_op jit(solution)/shard_map/ppermute | solution.py:15
  27.2 1.8 collective-permute-done.1
  29.5 0.7 fusion.35
  30.3 1.5 select_select_fusion
  32.2 4.7 copy.49
  36.9 6.1 %reshape.243 = bf16[8,2,49152]{2,1,0:T(2,128)(2,1)S(1)} reshape(bf16[4096,1,3,64]{3,2,1,0:T(4,128)(2,1)} %bitcast.77) | data formatting | bytes 3145728
  43.0 48.1 %all_to_all.15 = bf16[8,2,49152]{2,1,0:T(2,128)(2,1)S(1)} all-to-all(bf16[8,2,49152]{2,1,0:T(2,128)(2,1)S(1)} %reshape.243), channel_id=1, replica_groups=mesh['frame'=8,'tile'=32] {'frame'}, dimensions={0} | all-to-all | bytes 3145728 | tf_op jit(solution)/shard_map/all_to_all | solution.py:55
  91.2 4.8 reshape.244
  96.0 4.8 copy.67
  100.8 1.4 copy.51
  102.7 2.0 fusion.36
  104.9 2.1 convert_element_type.26
  107.3 0.8 copy.70
  108.2 248.2 %all-reduce.3.cloned.1.call-done = f32[512,512]{0,1:T(8,128)} async-done(((f32[512,512]{0,1:T(8,128)}), f32[512,512]{0,1:T(8,128)}) %all-reduce.3.cloned.1.call-update) | async-done | bytes 1048592 | tf_op jit(solution)/shard_map/psum | solution.py:61
  356.4 1.6 copy.53
  358.3 11.7 %cholesky.104 = f32[128,128]{1,0:T(8,128)S(1)} custom-call(f32[128,128]{1,0:T(8,128)S(1)} %cholesky.266), custom_call_target="Cholesky" | custom-call | tf_op jit(solution)/shard_map/jit(cholesky)/cholesky | solution.py:62
  370.2 9.8 %custom-call.30 = f32[1,128,128]{1,2,0:T(8,128)S(1)} custom-call(f32[1,128,128]{2,1,0:T(8,128)S(1)} %get-tuple-element.45), custom_call_target="InvertDiagBlocksLowerTriangular" | custom-call | tf_op jit(solution)/shard_map/jit(cholesky)/cholesky | solution.py:62
  380.7 11.8 %cholesky.217 = f32[128,128]{1,0:T(8,128)S(1)} custom-call(f32[128,128]{1,0:T(8,128)S(1)} %cholesky.270), custom_call_target="Cholesky" | custom-call | tf_op jit(solution)/shard_map/jit(cholesky)/cholesky | solution.py:62
  393.8 9.8 %custom-call.31 = f32[1,128,128]{1,2,0:T(8,128)S(1)} custom-call(f32[1,128,128]{2,1,0:T(8,128)S(1)} %get-tuple-element.42), custom_call_target="InvertDiagBlocksLowerTriangular" | custom-call | tf_op jit(solution)/shard_map/jit(cholesky)/cholesky | solution.py:62
  404.3 11.7 %cholesky.238 = f32[128,128]{1,0:T(8,128)S(1)} custom-call(f32[128,128]{1,0:T(8,128)S(1)} %cholesky.275), custom_call_target="Cholesky" | custom-call | tf_op jit(solution)/shard_map/jit(cholesky)/cholesky | solution.py:62
  416.1 0.7 compare_reduce_fusion.1
  416.7 9.8 %custom-call.32 = f32[1,128,128]{1,2,0:T(8,128)S(1)} custom-call(f32[1,128,128]{2,1,0:T(8,128)S(1)} %get-tuple-element.39), custom_call_target="InvertDiagBlocksLowerTriangular" | custom-call | tf_op jit(solution)/shard_map/jit(cholesky)/cholesky | solution.py:62
  427.1 11.9 %cholesky.255 = f32[128,128]{1,0:T(8,128)S(1)} custom-call(f32[128,128]{1,0:T(8,128)S(1)} %convolution_subtract_fusion.5), custom_call_target="Cholesky" | custom-call | tf_op jit(solution)/shard_map/jit(cholesky)/cholesky | solution.py:62
  439.1 0.7 compare_reduce_fusion
  442.6 10.0 %while.1 = (s32[]{:T(128)}, f32[512,512]{1,0:T(8,128)S(1)}, s32[4,2]{0,1:T(2,128)S(1)}, f32[4,128,128]{2,1,0:T(8,128)}, s32[]{:T(128)}) while((s32[]{:T(128)}, f32[512,512]{1,0:T(8,128)S(1)}, s32[4,2]{0,1:T(2,128)S(1)}, f32[4,128,128]{2,1,0:T(8,128)}, s32[]{:T(128)}) %tuple.39), condition=%wide.while_cond, body=%wide.while_body.sunk | while | flops 2 | bytes 132705 | solution.py:64
  443.2 1.9 bitcast_dynamic-update-slice_fusion.2
  445.7 1.9 bitcast_dynamic-update-slice_fusion.2
  448.2 1.9 bitcast_dynamic-update-slice_fusion.2
  450.7 1.9 bitcast_dynamic-update-slice_fusion.2
  452.6 40.2 %custom-call.33 = f32[4,128,128]{1,2,0:T(8,128)S(1)} custom-call(f32[4,128,128]{2,1,0:T(8,128)} %get-tuple-element.9), custom_call_target="InvertDiagBlocksLowerTriangular" | custom-call | tf_op jit(solution)/shard_map/triangular_solve | solution.py:64
  492.8 1.6 fusion.26
  494.4 2.1 convolution_subtract_fusion.2
  496.5 1.7 fusion.25
  498.3 1.9 convolution_subtract_fusion
  500.2 1.7 fusion.23
  501.9 3.4 fusion.1
  505.3 1.1 copy.57
  506.4 1.2 copy.56
  507.6 1.1 copy.55
  508.7 1.4 copy.58
  510.1 1.7 convolution_bitcast_fusion
  512.1 1.4 copy.61
  513.5 2.3 copy.60
  515.8 1.3 copy.64
  517.1 2.7 fusion.7
  (52 shorter events, 8.6 us)
Async XLA Ops:
  7.2 349.3 %all-reduce.3.cloned.1.call-start = ((), (), s32[]{:S(2)}) async-start(), calls=%async_computation.1 | async-start | bytes 2097152 | tf_op jit(solution)/shard_map/psum | solution.py:61
  9.0 18.2 %collective-permute-start = (bf16[64,2,1,4096]{3,0,2,1:T(8,128)(2,1)S(1)}, bf16[64,2,1,4096]{3,0,2,1:T(8,128)(2,1)S(1)}, u32[]{:S(2)}, u32[]{:S(2)}) collective-permute-start(bf16[64,2,1,4096]{3,0,2,1:T(8,128)(2,1)S(1)} %copy.46), channel_id=1, source_target_pairs={{0,1},{1,2},{2,3},{3,4},{4,5},{5,6},{6,7},{7,8},{8,9},{9,10},{10,1... | collective-permute-start | bytes 3145736 | tf_op jit(solution)/shard_map/ppermute | solution.py:15
  10.9 18.1 %collective-permute-start.1 = (bf16[64,2,1,4096]{3,0,2,1:T(8,128)(2,1)S(1)}, bf16[64,2,1,4096]{3,0,2,1:T(8,128)(2,1)S(1)}, u32[]{:S(2)}, u32[]{:S(2)}) collective-permute-start(bf16[64,2,1,4096]{3,0,2,1:T(8,128)(2,1)S(1)} %copy.46), channel_id=1, source_target_pairs={{1,0},{2,1},{3,2},{4,3},{5,4},{6,5},{7,6},{8,7},{9,8},{10,9},{11,1... | collective-permute-start | bytes 3145736 | tf_op jit(solution)/shard_map/ppermute | solution.py:16
  356.4 1.7 copy-start.1
  452.6 40.2 %copy-start.3 = (f32[512,512]{1,0:T(8,128)}, f32[512,512]{1,0:T(8,128)S(1)}, u32[]{:S(2)}) copy-start(f32[512,512]{1,0:T(8,128)S(1)} %get-tuple-element.100) | copy-start | bytes 3145732
  492.8 1.6 copy-start.4
  494.4 3.8 copy-start
  507.6 4.3 copy-start.2
Sparse Core Ops, SparseCore 0:
  104.8 251.5 all-reduce.2
where the time goes:
time: 532 us; the launch traced here: 527 us
  waiting for transfers between devices  261 us (49%)
  other arithmetic  127 us (24%)
  local copies, waits for them, and re-layouts  48.3 us (9%)
  blocking collectives  48.1 us (9%)
  matrix products  17.9 us (3%)
  between operations  17.2 us (3%)
  starting transfers between devices  7.71 us (1%)
    psum x1, waiting for transfers between devices, local(): gram = lax.psum(local_gram, ('frame', 'tile'))  248 us
    another operation x15, other arithmetic, local(): lower = jnp.linalg.cholesky(gram)  79.4 us
    all_to_all x1, blocking collectives, local(): lax.all_to_all(strain, 'frame', split_axis=3, concat_axis=0, tiled=True)  48.1 us
    another operation x2, other arithmetic, local(): lax.linalg.triangular_solve(lower, snapshot, left_side=True, lower=True)  40.2 us
    unnamed x16, local copies, waits for them, and re-layouts  15.4 us
    another operation x7, matrix products, local(): lax.linalg.triangular_solve(lower, snapshot, left_side=True, lower=True)  14.1 us
  transfers between devices with their start and end apart: 3, of which 3 were waited for; matrix products, arithmetic and copies ran while one was open for 1% of the time, Pallas kernels for 0%

commit v1 on v0

--- a/solution.py
+++ b/solution.py
@@ -3,6 +3,14 @@
 import jax.numpy as jnp
 from jax import lax
 from jax.sharding import PartitionSpec as P
+from jax.lax import all_to_all, psum
+
+
+def post_marks(obj, bus_axis):
+    item_now = all_to_all(
+        jnp.stack(jnp.split(obj, psum(1, bus_axis), axis=3), axis=0), bus_axis, 0, 0
+    )
+    return jnp.concatenate(item_now, 0)
 
 
 def with_halo(array, sides, width):
@@ -52,7 +60,7 @@
     d_rows = derivative(center, field[:, :, :-2, :], field[:, :, 2:, :], first, final)
     d_cols = column_derivative(center)
     strain = combine_strain(d_rows, d_cols)
-    pixel_major = lax.all_to_all(strain, "frame", split_axis=3, concat_axis=0, tiled=True)
+    pixel_major = post_marks(strain, bus_axis="frame")
     frames = pixel_major.shape[0]
     snapshot_half = pixel_major.reshape(frames, -1)
     local_gram = lax.dot_general(

time: 532 us -> 510 us (0.959)
  local copies, waits for them, and re-layouts: 48.3 us -> 27.2 us
    unnamed x16 -> x21, local copies, waits for them, and re-layouts: 15.4 us -> 4.04 us
where the time goes in v1:
time: 510 us; the launch traced here: 506 us
  waiting for transfers between devices  262 us (51%)
  other arithmetic  127 us (25%)
  blocking collectives  48.1 us (9%)
  local copies, waits for them, and re-layouts  27.2 us (5%)
  between operations  17.2 us (3%)
  matrix products  16.8 us (3%)
  starting transfers between devices  7.71 us (2%)
    psum x1, waiting for transfers between devices, local(): gram = lax.psum(local_gram, ('frame', 'tile'))  249 us
    another operation x15, other arithmetic, local(): lower = jnp.linalg.cholesky(gram)  79.4 us
    all_to_all x1, blocking collectives, post_marks(): all_to_all(jnp.stack(jnp.split(obj, psum(1, bus_axis), axis=3), axis=0),...  48.1 us
    another operation x2, other arithmetic, local(): lax.linalg.triangular_solve(lower, snapshot, left_side=True, lower=True)  40.2 us
    another operation x7, matrix products, local(): lax.linalg.triangular_solve(lower, snapshot, left_side=True, lower=True)  12.9 us
    ppermute x1, waiting for transfers between devices, with_halo(): before = lax.ppermute(last, axis, up)  10.5 us
  transfers between devices with their start and end apart: 3, of which 3 were waited for; matrix products, arithmetic and copies ran while one was open for 1% of the time, Pallas kernels for 0%

profile of v1, /device:TPU:2, one launch (start us, length us, event | category | flops | bytes accessed | tf_op | source)
XLA Modules:
  0.0 505.9 jit_solution(11377246017575653846)
XLA Ops:
  7.2 1.8 copy.38
  9.0 1.9 collective-permute-start
  10.9 5.8 %collective-permute-start.1 = (bf16[64,2,1,4096]{3,0,1,2:T(8,128)(2,1)S(1)}, bf16[64,2,1,4096]{3,0,1,2:T(8,128)(2,1)S(1)}, u32[]{:S(2)}, u32[]{:S(2)}) collective-permute-start(bf16[64,2,1,4096]{3,0,1,2:T(8,128)(2,1)S(1)} %copy.38), channel_id=1, source_target_pairs={{1,0},{2,1},{3,2},{4,3},{5,4},{6,5},{7,6},{8,7},{9,8},{10,9},{11,1... | collective-permute-start | bytes 3145736 | tf_op jit(solution)/shard_map/ppermute | solution.py:24
  16.7 10.5 %collective-permute-done = bf16[64,2,1,4096]{3,0,1,2:T(8,128)(2,1)S(1)} collective-permute-done((bf16[64,2,1,4096]{3,0,1,2:T(8,128)(2,1)S(1)}, bf16[64,2,1,4096]{3,0,1,2:T(8,128)(2,1)S(1)}, u32[]{:S(2)}, u32[]{:S(2)}) %collective-permute-start) | collective-permute-done | bytes 1048608 | tf_op jit(solution)/shard_map/ppermute | solution.py:23
  27.2 1.8 collective-permute-done.1
  29.5 0.7 fusion.43
  30.3 1.5 select_select_fusion
  32.4 48.1 %all_to_all.5 = bf16[8,64,3,1,512]{4,1,3,2,0:T(8,128)(2,1)S(1)} all-to-all(bf16[8,64,3,1,512]{4,1,3,2,0:T(8,128)(2,1)S(1)} %fusion.20), channel_id=1, replica_groups=mesh['frame'=8,'tile'=32] {'frame'}, dimensions={0} | all-to-all | bytes 3145728 | tf_op jit(solution)/shard_map/all_to_all | solution.py:10
  80.5 1.4 copy.48
  81.9 0.5 copy.65
  82.4 2.0 fusion.44
  84.4 2.1 convert_element_type.26
  87.0 249.3 %all-reduce.3.cloned.1.call-done = f32[512,512]{0,1:T(8,128)} async-done(((f32[512,512]{0,1:T(8,128)}), f32[512,512]{0,1:T(8,128)}) %all-reduce.3.cloned.1.call-update) | async-done | bytes 1048592 | tf_op jit(solution)/shard_map/psum | solution.py:69
  336.3 1.6 copy.50
  338.2 11.7 %cholesky.104 = f32[128,128]{1,0:T(8,128)S(1)} custom-call(f32[128,128]{1,0:T(8,128)S(1)} %cholesky.266), custom_call_target="Cholesky" | custom-call | tf_op jit(solution)/shard_map/jit(cholesky)/cholesky | solution.py:70
  350.1 9.8 %custom-call.30 = f32[1,128,128]{1,2,0:T(8,128)S(1)} custom-call(f32[1,128,128]{2,1,0:T(8,128)S(1)} %get-tuple-element.43), custom_call_target="InvertDiagBlocksLowerTriangular" | custom-call | tf_op jit(solution)/shard_map/jit(cholesky)/cholesky | solution.py:70
  360.6 11.9 %cholesky.217 = f32[128,128]{1,0:T(8,128)S(1)} custom-call(f32[128,128]{1,0:T(8,128)S(1)} %cholesky.270), custom_call_target="Cholesky" | custom-call | tf_op jit(solution)/shard_map/jit(cholesky)/cholesky | solution.py:70
  372.5 0.6 compare_reduce_fusion.2
  373.1 0.6 compare_reduce_fusion.3
  373.8 9.8 %custom-call.31 = f32[1,128,128]{1,2,0:T(8,128)S(1)} custom-call(f32[1,128,128]{2,1,0:T(8,128)S(1)} %get-tuple-element.40), custom_call_target="InvertDiagBlocksLowerTriangular" | custom-call | tf_op jit(solution)/shard_map/jit(cholesky)/cholesky | solution.py:70
  384.2 11.7 %cholesky.238 = f32[128,128]{1,0:T(8,128)S(1)} custom-call(f32[128,128]{1,0:T(8,128)S(1)} %cholesky.275), custom_call_target="Cholesky" | custom-call | tf_op jit(solution)/shard_map/jit(cholesky)/cholesky | solution.py:70
  396.0 0.7 compare_reduce_fusion.1
  396.6 9.8 %custom-call.32 = f32[1,128,128]{1,2,0:T(8,128)S(1)} custom-call(f32[1,128,128]{2,1,0:T(8,128)S(1)} %get-tuple-element.37), custom_call_target="InvertDiagBlocksLowerTriangular" | custom-call | tf_op jit(solution)/shard_map/jit(cholesky)/cholesky | solution.py:70
  407.0 11.9 %cholesky.255 = f32[128,128]{1,0:T(8,128)S(1)} custom-call(f32[128,128]{1,0:T(8,128)S(1)} %convolution_subtract_fusion.5), custom_call_target="Cholesky" | custom-call | tf_op jit(solution)/shard_map/jit(cholesky)/cholesky | solution.py:70
  419.0 0.7 compare_reduce_fusion
  422.5 10.0 %while.1 = (s32[]{:T(128)}, f32[512,512]{1,0:T(8,128)S(1)}, s32[4,2]{0,1:T(2,128)S(1)}, f32[4,128,128]{2,1,0:T(8,128)}, s32[]{:T(128)}) while((s32[]{:T(128)}, f32[512,512]{1,0:T(8,128)S(1)}, s32[4,2]{0,1:T(2,128)S(1)}, f32[4,128,128]{2,1,0:T(8,128)}, s32[]{:T(128)}) %tuple.38), condition=%wide.while_cond, body=%wide.while_body.sunk | while | flops 2 | bytes 132705 | solution.py:72
  422.6 0.5 fusion.54
  423.1 1.9 bitcast_dynamic-update-slice_fusion.2
  425.1 0.5 fusion.54
  425.6 1.9 bitcast_dynamic-update-slice_fusion.2
  427.6 0.5 fusion.54
  428.1 1.9 bitcast_dynamic-update-slice_fusion.2
  430.6 1.9 bitcast_dynamic-update-slice_fusion.2
  432.5 40.2 %custom-call.33 = f32[4,128,128]{1,2,0:T(8,128)S(1)} custom-call(f32[4,128,128]{2,1,0:T(8,128)} %get-tuple-element.9), custom_call_target="InvertDiagBlocksLowerTriangular" | custom-call | tf_op jit(solution)/shard_map/triangular_solve | solution.py:72
  473.4 2.1 convolution_subtract_fusion.2
  475.5 1.7 fusion.33
  477.2 1.9 convolution_subtract_fusion
  479.1 1.7 fusion.31
  480.8 3.4 fusion.1
  484.2 1.1 copy.54
  485.4 1.2 copy.53
  486.5 1.1 copy.52
  487.7 1.4 copy.55
  489.1 1.7 convolution_bitcast_fusion
  491.1 1.4 copy.58
  492.5 2.3 copy.57
  494.8 1.3 copy.61
  496.1 2.7 fusion.7
  (56 shorter events, 6.0 us)
Async XLA Ops:
  7.2 329.2 %all-reduce.3.cloned.1.call-start = ((), (), s32[]{:S(2)}) async-start(), calls=%async_computation.1 | async-start | bytes 2097152 | tf_op jit(solution)/shard_map/psum | solution.py:69
  9.0 18.2 %collective-permute-start = (bf16[64,2,1,4096]{3,0,1,2:T(8,128)(2,1)S(1)}, bf16[64,2,1,4096]{3,0,1,2:T(8,128)(2,1)S(1)}, u32[]{:S(2)}, u32[]{:S(2)}) collective-permute-start(bf16[64,2,1,4096]{3,0,1,2:T(8,128)(2,1)S(1)} %copy.38), channel_id=1, source_target_pairs={{0,1},{1,2},{2,3},{3,4},{4,5},{5,6},{6,7},{7,8},{8,9},{9,10},{10,1... | collective-permute-start | bytes 3145736 | tf_op jit(solution)/shard_map/ppermute | solution.py:23
  10.9 18.1 %collective-permute-start.1 = (bf16[64,2,1,4096]{3,0,1,2:T(8,128)(2,1)S(1)}, bf16[64,2,1,4096]{3,0,1,2:T(8,128)(2,1)S(1)}, u32[]{:S(2)}, u32[]{:S(2)}) collective-permute-start(bf16[64,2,1,4096]{3,0,1,2:T(8,128)(2,1)S(1)} %copy.38), channel_id=1, source_target_pairs={{1,0},{2,1},{3,2},{4,3},{5,4},{6,5},{7,6},{8,7},{9,8},{10,9},{11,1... | collective-permute-start | bytes 3145736 | tf_op jit(solution)/shard_map/ppermute | solution.py:24
  336.3 1.7 copy-start.1
  432.5 40.7 %copy-start.3 = (f32[512,512]{1,0:T(8,128)}, f32[512,512]{1,0:T(8,128)S(1)}, u32[]{:S(2)}) copy-start(f32[512,512]{1,0:T(8,128)S(1)} %get-tuple-element.98) | copy-start | bytes 3145732
  472.7 0.7 copy-start.4
  473.4 3.8 copy-start
  486.5 4.3 copy-start.2
Sparse Core Ops, SparseCore 0:
  84.5 251.7 all-reduce.2
